TPU v7x, 32 devices: a whole 2x2x4 slice. The times are simulated.
32 devices in a mesh: clip: 8 (over z, x), tm: 4 (over y, core).
Axes of the slice: x: 2, y: 2, z: 4, core: 2. Of those that a mesh axis runs over, the one named last changes fastest.
Arguments:
- features: bfloat16 [16, 1024, 512], P('clip', 'tm'), may hold values from -6 to 6
- cotangent: bfloat16 [16, 1024, 512], P('clip', 'tm'), may hold values from -6 to 6
- clip_lengths: int32 [16], P('clip'), may hold values from 128 to 1024, as said below
- code_ids: int32 [4, 16, 1024], P(None, 'clip', 'tm'), may hold values from 0 to 1023
- step_count: int32 [1], replicated, may hold values from 2 to 20
- dilated_kernel_weight: float32 [3, 512, 256], P(None, None, 'clip'), may hold values from -0.15625 to 0.15625
- pointwise_conv: float32 [256, 512], P(None, 'clip'), may hold values from -0.75 to 0.75
- codebooks: float32 [4, 1024, 256], P(None, 'clip'), may hold values from -6 to 6
- dilated_first_moment: float32 [3, 512, 256], P(None, None, 'clip'), may hold values from -1 to 1
- dilated_second_moment: float32 [3, 512, 256], P(None, None, 'clip'), may hold values from 0.028995216 to 0.11598086
- pointwise_first: float32 [256, 512], P(None, 'clip'), may hold values from -1 to 1
- pointwise_second: float32 [256, 512], P(None, 'clip'), may hold values from 0.028995216 to 0.11598086
- codebook_first: float32 [4, 1024, 256], P(None, 'clip'), may hold values from -0.01953125 to 0.01953125
- codebook_second: float32 [4, 1024, 256], P(None, 'clip'), may hold values from 9.745614e-06 to 3.8982456e-05
Outputs:
- quantized: bfloat16 [16, 1024, 512], P('clip', 'tm')
- features_gradient: float32 [16, 1024, 512], P('clip', 'tm')
- grad_norm: float32 [1], replicated
- dilated_new: float32 [3, 512, 256], P(None, None, 'clip')
- dilated_grad: float32 [3, 512, 256], P(None, None, 'clip')
- dilated_square: float32 [3, 512, 256], P(None, None, 'clip')
- pointwise_new: float32 [256, 512], P(None, 'clip')
- pointwise_grad: float32 [256, 512], P(None, 'clip')
- pointwise_square: float32 [256, 512], P(None, 'clip')
- codebook_new: float32 [4, 1024, 256], P(None, 'clip')
- codebook_grad: float32 [4, 1024, 256], P(None, 'clip')
- codebook_square: float32 [4, 1024, 256], P(None, 'clip')
Inputs may be any that keep to these rules, and one draw needn't show every extreme that they name: `clip_lengths`: the number of valid frames of each clip; frames from it on are padding; clip 0 is always full.
All inputs are finite; a program needn't handle non-finite values.
Results may differ from a plain program's by a relative error of at most 0.001.
The roundings to bfloat16 on the way count: a program that leaves them out, or rounds other values in their place, can miss the bound.
Values may be sent and summed in bfloat16 or wider, within the bound.
No kernel may reach another device: no remote copies, remote signals or barrier semaphores. Data moves between devices by JAX's collectives and lax.ppermute only.
A program may use at most 64 MiB of HBM per device.

v0:
```python
import jax
import jax.numpy as jnp
from jax import lax
from jax.sharding import PartitionSpec as P

HID = 256
CODES = 1024
GROUPS = 2
LEVELS = 2
KERNEL = 3
DILATION = 3
DG = 256
COMMIT = 0.25
FIRST_DECAY = 0.9
SECOND_DECAY = 0.99
EPSILON = 1e-08
WEIGHT_DECAY = 0.01
BITRATE_FACTOR = 0.02
RATE_CODE = 0.5


def extended(cells, sides, width):
    for axis, dim in sides:
        count = lax.axis_size(axis)
        ends = count - 1
        head = lax.slice_in_dim(cells, 0, width, axis=dim)
        tail = lax.slice_in_dim(cells, cells.shape[dim] - width, cells.shape[dim], axis=dim)
        cells = jnp.concatenate(
            [
                lax.ppermute(tail, axis, [(i, (i + 1) % count) for i in range(ends)]),
                cells,
                lax.ppermute(head, axis, [((i + 1) % count, i) for i in range(ends)]),
            ],
            axis=dim,
        )
    return cells


def elu_slope(values):
    return jnp.where(values > 0, 1.0, jnp.exp(jnp.minimum(values, 0.0)))


def adamw_update(weight, first, second, grad, rate, completed_steps):
    first_new = FIRST_DECAY * first + (1.0 - FIRST_DECAY) * grad
    second_new = SECOND_DECAY * second + (1.0 - SECOND_DECAY) * grad * grad
    first_hat = first_new / (1.0 - FIRST_DECAY**completed_steps)
    second_hat = second_new / (1.0 - SECOND_DECAY**completed_steps)
    weight_new = weight - rate * (
        first_hat / (jnp.sqrt(second_hat) + EPSILON) + WEIGHT_DECAY * weight
    )
    return (weight_new, grad, second_new)


def shards(
    features,
    cotangent,
    clip_lengths,
    code_ids,
    step_count,
    dilated_kernel_weight,
    pointwise_conv,
    codebooks,
    dilated_first_moment,
    dilated_second_moment,
    pointwise_first,
    pointwise_second,
    codebook_first,
    codebook_second,
):
    clip_rank = lax.axis_index("clip")
    time_rank = lax.axis_index("tm")
    dilated_full, pointwise_full, table_full = (
        lax.all_gather(dilated_kernel_weight.astype(jnp.bfloat16), "clip", axis=2, tiled=True),
        lax.all_gather(pointwise_conv.astype(jnp.bfloat16), "clip", axis=1, tiled=True),
        lax.all_gather(codebooks.astype(jnp.bfloat16), "clip", axis=1, tiled=True),
    )
    clips, frames, width = features.shape
    positions = time_rank * frames + lax.broadcasted_iota(jnp.int32, (clips, frames, 1), 1)
    frame_mask = (positions < clip_lengths[:, None, None]).astype(jnp.float32)
    start = features.astype(jnp.float32) * frame_mask
    activated = jax.nn.elu(start).astype(jnp.bfloat16)
    padded = extended(activated, (("tm", 1),), DILATION)
    hidden = jnp.zeros((clips, frames, HID), jnp.float32)
    for tap_index in range(KERNEL):
        window = padded[:, tap_index * DILATION : tap_index * DILATION + frames]
        hidden = hidden + jnp.einsum(
            "btc,cd->btd", window, dilated_full[tap_index], preferred_element_type=jnp.float32
        )
    gated = jax.nn.elu(hidden).astype(jnp.bfloat16)
    latent = start + jnp.einsum(
        "btk,kd->btd", gated, pointwise_full, preferred_element_type=jnp.float32
    )
    backs = cotangent.astype(jnp.float32) * frame_mask
    latent_parts = []
    quant_parts = []
    table_grads = []
    for group in range(GROUPS):
        residual_part = latent[..., group * DG : (group + 1) * DG]
        moving_grad = backs[..., group * DG : (group + 1) * DG]
        summed = jnp.zeros_like(residual_part)
        for level in range(LEVELS):
            slot = group * LEVELS + level
            chosen = jnp.take(table_full[slot], code_ids[slot], axis=0).astype(jnp.float32)
            moving_grad = moving_grad + 2.0 * COMMIT * frame_mask * (residual_part - chosen)
            code_grad = 2.0 * frame_mask * (chosen - residual_part)
            table_grads.append(
                jax.ops.segment_sum(
                    code_grad.reshape(-1, DG), code_ids[slot].reshape(-1), num_segments=CODES
                )
            )
            residual_part = residual_part - chosen
            summed = summed + chosen
        latent_parts.append(moving_grad)
        quant_parts.append(summed)
    quantized = (jnp.concatenate(quant_parts, axis=-1) * frame_mask).astype(jnp.bfloat16)
    latent_grad = jnp.concatenate(latent_parts, axis=-1)
    table_grad = jnp.stack(table_grads, axis=0)
    branch_grad = latent_grad.astype(jnp.bfloat16)
    pointwise_grad = jnp.einsum(
        "btk,btd->kd", gated, branch_grad, preferred_element_type=jnp.float32
    )
    gated_grad = jnp.einsum(
        "btd,kd->btk", branch_grad, pointwise_full, preferred_element_type=jnp.float32
    )
    hidden_grad = (gated_grad * elu_slope(hidden)).astype(jnp.bfloat16)
    padded_grad = extended(hidden_grad, (("tm", 1),), DILATION)
    dilated_parts = []
    act_grad = jnp.zeros((clips, frames, width), jnp.float32)
    for tap_index in range(KERNEL):
        window = padded[:, tap_index * DILATION : tap_index * DILATION + frames]
        dilated_parts.append(
            jnp.einsum("btc,btd->cd", window, hidden_grad, preferred_element_type=jnp.float32)
        )
        offset = (KERNEL - 1 - tap_index) * DILATION
        act_grad = act_grad + jnp.einsum(
            "btd,cd->btc",
            padded_grad[:, offset : offset + frames],
            dilated_full[tap_index],
            preferred_element_type=jnp.float32,
        )
    dilated_grad = jnp.stack(dilated_parts, axis=0)
    features_gradient = frame_mask * (latent_grad + elu_slope(start) * act_grad)
    local_grads = (dilated_grad, pointwise_grad, table_grad)
    whole = lax.psum((local_grads[0], local_grads[1], local_grads[2]), ("clip", "tm"))
    squared = sum((jnp.sum(piece * piece) for piece in whole))
    shares = (
        lax.dynamic_slice_in_dim(
            whole[0], clip_rank * dilated_kernel_weight.shape[2], dilated_kernel_weight.shape[2], 2
        ),
        lax.dynamic_slice_in_dim(
            whole[1], clip_rank * pointwise_conv.shape[1], pointwise_conv.shape[1], 1
        ),
        lax.dynamic_slice_in_dim(whole[2], clip_rank * codebooks.shape[1], codebooks.shape[1], 1),
    )
    count = dilated_full.size + pointwise_full.size + table_full.size
    limit = jnp.sqrt(jnp.float32(count))
    gradient_norm_total = jnp.sqrt(squared)
    clip_scale_factor = limit / jnp.maximum(gradient_norm_total, limit)
    completed_steps = step_count[0].astype(jnp.float32)
    dilation_factor = adamw_update(
        dilated_kernel_weight,
        dilated_first_moment,
        dilated_second_moment,
        shares[0] * clip_scale_factor,
        BITRATE_FACTOR,
        completed_steps,
    )
    pointwise_kernel = adamw_update(
        pointwise_conv,
        pointwise_first,
        pointwise_second,
        shares[1] * clip_scale_factor,
        BITRATE_FACTOR,
        completed_steps,
    )
    codebook_tensor = adamw_update(
        codebooks,
        codebook_first,
        codebook_second,
        shares[2] * clip_scale_factor,
        RATE_CODE,
        completed_steps,
    )
    return (
        quantized,
        features_gradient,
        gradient_norm_total.reshape(1),
        dilation_factor[0],
        dilation_factor[1],
        dilation_factor[2],
        pointwise_kernel[0],
        pointwise_kernel[1],
        pointwise_kernel[2],
        codebook_tensor[0],
        codebook_tensor[1],
        codebook_tensor[2],
    )


def solution(mesh):
    in_specs = (
        P("clip", "tm", None),
        P("clip", "tm", None),
        P("clip"),
        P(None, "clip", "tm"),
        P(),
        P(None, None, "clip"),
        P(None, "clip"),
        P(None, "clip", None),
        P(None, None, "clip"),
        P(None, None, "clip"),
        P(None, "clip"),
        P(None, "clip"),
        P(None, "clip", None),
        P(None, "clip", None),
    )
    out_specs = (
        P("clip", "tm", None),
        P("clip", "tm", None),
        P(),
        P(None, None, "clip"),
        P(None, None, "clip"),
        P(None, None, "clip"),
        P(None, "clip"),
        P(None, "clip"),
        P(None, "clip"),
        P(None, "clip", None),
        P(None, "clip", None),
        P(None, "clip", None),
    )
    return jax.shard_map(shards, mesh=mesh, in_specs=in_specs, out_specs=out_specs, check_vma=False)
```

profile of v0, /device:TPU:0, one launch (start us, length us, event | category | flops | bytes accessed | tf_op | source)
XLA Modules:
  0.0 310.3 jit_solution(5738353770341371367)
XLA Ops:
  7.2 1.8 convert_element_type.54
  9.8 2.8 convert_multiply_fusion.1
  12.7 1.3 collective-permute-start.1
  14.0 3.0 collective-permute-start
  17.8 0.9 convert_element_type.64
  19.6 33.2 %all_gather.11 = bf16[256,512]{0,1:T(8,128)(2,1)S(1)} all-gather(bf16[256,64]{0,1:T(8,128)(2,1)S(1)} %convert_element_type.66), channel_id=1, replica_groups=mesh['clip'=8,'tm'=4] {'clip'}, dimensions={1}, use_global_device_ids=true | all-gather | bytes 294912 | tf_op jit(solution)/shard_map/all_gather | solution.py:74
  52.9 33.2 %all_gather.10 = bf16[3,512,256]{1,2,0:T(8,128)(2,1)S(1)} all-gather(bf16[3,512,32]{1,2,0:T(8,128)(2,1)S(1)} %convert_element_type.64), channel_id=1, replica_groups=mesh['clip'=8,'tm'=4] {'clip'}, dimensions={2}, use_global_device_ids=true | all-gather | bytes 884736 | tf_op jit(solution)/shard_map/all_gather | solution.py:73
  88.0 1.4 convolution_add_fusion.1
  89.4 1.7 slice_bitcast_fusion.3
  91.1 2.6 gather_fusion.1
  93.7 2.6 gather_fusion
  96.2 2.6 gather_fusion.3
  98.8 1.9 gather_fusion.2
  100.8 3.3 %fusion.12 = (f32[2,256,256]{2,1,0:T(8,128)S(1)}, f32[2,256,256]{2,1,0:T(8,128)S(1)}, f32[2,256,256]{2,1,0:T(8,128)}, f32[2,256,256]{2,1,0:T(8,128)}, f32[2,256,...) fusion(f32[2,256,512]{2,1,0:T(8,128)S(1)} %copy-done, ...), kind=kLoop, calls=%fused_computation.50 | loop fusion | flops 3932160 | bytes 7346176 | tf_op jit(solution)/shard_map/add | solution.py:104
  104.4 1.3 convolution_bitcast_fusion
  106.1 4.2 %scatter_custom_fusion.3 = f32[1024,256]{1,0:T(8,128)S(1)} fusion(s32[512]{0:T(512)S(1)} %bitcast.135, f32[512,256]{1,0:T(8,128)} %bitcast.127, f32[]{:T(128)} %constant.35.clone.1), kind=kCustom, calls=%fused_computation.74 | custom fusion | flops 131072 | bytes 1049088 | tf_op jit(solution)/shard_map/scatter-add | solution.py:107
  110.4 4.8 %scatter_custom_fusion.2 = f32[1024,256]{1,0:T(8,128)} fusion(s32[512]{0:T(512)S(1)} %bitcast.134, f32[512,256]{1,0:T(8,128)} %bitcast.126, f32[]{:T(128)} %constant.35.clone.1), kind=kCustom, calls=%fused_computation.76 | custom fusion | flops 131072 | bytes 1049088 | tf_op jit(solution)/shard_map/scatter-add | solution.py:107
  115.1 4.8 %scatter_custom_fusion.1 = f32[1024,256]{1,0:T(8,128)} fusion(s32[512]{0:T(512)S(1)} %bitcast.133, f32[512,256]{1,0:T(8,128)} %bitcast.125, f32[]{:T(128)} %constant.35.clone.1), kind=kCustom, calls=%fused_computation.78 | custom fusion | flops 131072 | bytes 1049088 | tf_op jit(solution)/shard_map/scatter-add | solution.py:107
  119.9 4.8 %scatter_custom_fusion = f32[1024,256]{1,0:T(8,128)} fusion(s32[512]{0:T(512)S(1)} %bitcast.132, f32[512,256]{1,0:T(8,128)} %bitcast.124, f32[]{:T(128)} %constant.35.clone.1), kind=kCustom, calls=%fused_computation.80 | custom fusion | flops 131072 | bytes 1049088 | tf_op jit(solution)/shard_map/scatter-add | solution.py:107
  125.4 1.3 pad_maximum_fusion.1
  126.8 2.3 pad_maximum_fusion
  130.0 1.4 collective-permute-start.3
  131.4 1.5 collective-permute-start.2
  134.5 1.4 collective-permute-done.2
  136.0 1.6 fusion.3
  137.6 149.0 %all-reduce.3.cloned.1.call-done = (f32[3,512,256]{1,2,0:T(8,128)}, f32[256,512]{0,1:T(8,128)}, f32[4,1024,256]{2,1,0:T(8,128)}) async-done(((f32[3,512,256]{1,2,0:T(8,128)}, f32[256,512]{0,1:T(8,128)}, f32[4,1024,256]{2,1,0:T(8,128)}), (f32[3,512,256]{1,2,0:T(8,128)}, f32[256,512]{0,1:T(8,128)}, f32[4,1024,256]{2,1,0:T(8,128)})) %all-reduce.3.cloned.1.call-update) | async-done | bytes 6291472 | tf_op jit(solution)/shard_map/psum | solution.py:144
  286.6 2.4 multiply_reduce_fusion.1
  289.0 1.8 multiply_reduce_fusion.2
  290.8 3.9 %multiply_reduce_fusion = f32[]{:T(128)} fusion(f32[4,1024,256]{2,1,0:T(8,128)} %get-tuple-element.39), kind=kLoop, calls=%fused_computation.9 | loop fusion | flops 2097151 | bytes 4194308 | tf_op jit(solution)/shard_map/reduce_sum | solution.py:145
  296.7 1.8 multiply_subtract_fusion.1
  298.5 1.5 multiply_subtract_fusion.2
  300.1 2.3 multiply_subtract_fusion
  (93 shorter events, 7.4 us)
Async XLA Ops:
  7.2 45.6 %copy-start.26 = (s32[2]{0:T(128)S(1)}, s32[2]{0:T(128)}, u32[]{:S(2)}) copy-start(s32[2]{0:T(128)} %param.18) | copy-start | bytes 28
  7.2 45.7 %copy-start.23 = (s32[4,2,256]{2,1,0:T(2,128)S(1)}, s32[4,2,256]{2,1,0:T(2,128)}, u32[]{:S(2)}) copy-start(s32[4,2,256]{2,1,0:T(2,128)} %param.19) | copy-start | bytes 24580
  7.2 82.2 %all-gather.2.cloned.1.call-start = ((), (), s32[]{:S(2)}) async-start(), calls=%async_computation | async-start | bytes 2359296 | tf_op jit(solution)/shard_map/all_gather | solution.py:75
  9.0 277.5 %all-reduce.3.cloned.1.call-start = ((), (), s32[]{:S(2)}) async-start(), calls=%async_computation.1 | async-start | bytes 12582912 | tf_op jit(solution)/shard_map/psum | solution.py:144
  9.8 78.2 %copy-start.11 = (bf16[2,256,512]{2,1,0:T(8,128)(2,1)S(1)}, bf16[2,256,512]{2,1,0:T(8,128)(2,1)}, u32[]{:S(2)}) copy-start(bf16[2,256,512]{2,1,0:T(8,128)(2,1)} %param.16) | copy-start | bytes 1572868
  12.7 73.8 %collective-permute-start.1 = (bf16[2,3,512]{2,1,0:T(4,128)(2,1)S(1)}, bf16[2,3,512]{2,1,0:T(4,128)(2,1)S(1)}, u32[]{:S(2)}, u32[]{:S(2)}) collective-permute-start(bf16[2,3,512]{2,1,0:T(4,128)(2,1)S(1)} %get-tuple-element.62), channel_id=1, source_target_pairs={{1,0},{2,1},{3,2},{5,4},{6,5},{7,6},{9,8},{10,9},{11,10},{13,12},{... | collective-permute-start | bytes 18440 | tf_op jit(solution)/shard_map/ppermute | solution.py:32
  14.0 72.9 %collective-permute-start = (bf16[2,3,512]{2,1,0:T(4,128)(2,1)S(1)}, bf16[2,3,512]{2,1,0:T(4,128)(2,1)S(1)}, u32[]{:S(2)}, u32[]{:S(2)}) collective-permute-start(bf16[2,3,512]{2,1,0:T(4,128)(2,1)S(1)} %get-tuple-element.61), channel_id=1, source_target_pairs={{0,1},{1,2},{2,3},{4,5},{5,6},{6,7},{8,9},{9,10},{10,11},{12,13},{... | collective-permute-start | bytes 18440 | tf_op jit(solution)/shard_map/ppermute | solution.py:30
  52.8 34.4 %copy-start.19 = (bf16[256,512]{0,1:T(8,128)(2,1)}, bf16[256,512]{0,1:T(8,128)(2,1)S(1)}, u32[]{:S(2)}) copy-start(bf16[256,512]{0,1:T(8,128)(2,1)S(1)} %all_gather.11) | copy-start | bytes 786436
  96.2 4.5 %copy-start = (f32[2,256,512]{2,1,0:T(8,128)S(1)}, f32[2,256,512]{2,1,0:T(8,128)}, u32[]{:S(2)}) copy-start(f32[2,256,512]{2,1,0:T(8,128)} %get-tuple-element.77) | copy-start | bytes 3145732
  100.8 3.3 %copy-start.17 = (f32[2,256,256]{2,1,0:T(8,128)S(1)}, f32[2,256,256]{2,1,0:T(8,128)}, u32[]{:S(2)}) copy-start(f32[2,256,256]{2,1,0:T(8,128)} %copy-done.16) | copy-start | bytes 1572868
  100.8 3.3 %copy-start.20 = (bf16[256,512]{0,1:T(8,128)(2,1)S(1)}, bf16[256,512]{0,1:T(8,128)(2,1)}, u32[]{:S(2)}) copy-start(bf16[256,512]{0,1:T(8,128)(2,1)} %copy-done.19) | copy-start | bytes 786436
  104.1 2.0 copy-start.7
  104.1 2.0 copy-start.9
  124.7 2.0 copy-start.1
  124.7 2.0 copy-start.2
  124.7 2.0 copy-start.3
  129.0 4.2 %copy-start.5 = (f32[2,256,256]{2,1,0:T(8,128)S(1)}, f32[2,256,256]{2,1,0:T(8,128)}, u32[]{:S(2)}) copy-start(f32[2,256,256]{2,1,0:T(8,128)} %get-tuple-element.59) | copy-start | bytes 1572868
  129.1 4.2 %copy-start.6 = (f32[2,256,256]{2,1,0:T(8,128)S(1)}, f32[2,256,256]{2,1,0:T(8,128)}, u32[]{:S(2)}) copy-start(f32[2,256,256]{2,1,0:T(8,128)} %get-tuple-element.60) | copy-start | bytes 1572868
  129.1 6.9 %copy-start.8 = (f32[2,256,256]{2,1,0:T(8,128)S(1)}, f32[2,256,256]{2,1,0:T(8,128)}, u32[]{:S(2)}) copy-start(f32[2,256,256]{2,1,0:T(8,128)} %copy-done.7) | copy-start | bytes 1572868
  129.1 6.9 %copy-start.10 = (f32[2,256,256]{2,1,0:T(8,128)S(1)}, f32[2,256,256]{2,1,0:T(8,128)}, u32[]{:S(2)}) copy-start(f32[2,256,256]{2,1,0:T(8,128)} %copy-done.9) | copy-start | bytes 1572868
  130.0 6.0 %copy-start.12 = (bf16[2,256,512]{2,1,0:T(8,128)(2,1)S(1)}, bf16[2,256,512]{2,1,0:T(8,128)(2,1)}, u32[]{:S(2)}) copy-start(bf16[2,256,512]{2,1,0:T(8,128)(2,1)} %param.16) | copy-start | bytes 1572868
  130.0 4.2 %collective-permute-start.3 = (bf16[2,3,256]{2,1,0:T(4,128)(2,1)S(1)}, bf16[2,3,256]{2,1,0:T(4,128)(2,1)S(1)}, u32[]{:S(2)}, u32[]{:S(2)}) collective-permute-start(bf16[2,3,256]{2,1,0:T(4,128)(2,1)S(1)} %get-tuple-element.64), channel_id=1, source_target_pairs={{0,1},{1,2},{2,3},{4,5},{5,6},{6,7},{8,9},{9,10},{10,11},{12,13},{... | collective-permute-start | bytes 9224 | tf_op jit(solution)/shard_map/ppermute | solution.py:30
  131.4 4.5 %collective-permute-start.2 = (bf16[2,3,256]{2,1,0:T(4,128)(2,1)S(1)}, bf16[2,3,256]{2,1,0:T(4,128)(2,1)S(1)}, u32[]{:S(2)}, u32[]{:S(2)}) collective-permute-start(bf16[2,3,256]{2,1,0:T(4,128)(2,1)S(1)} %get-tuple-element.63), channel_id=1, source_target_pairs={{1,0},{2,1},{3,2},{5,4},{6,5},{7,6},{9,8},{10,9},{11,10},{13,12},{... | collective-permute-start | bytes 9224 | tf_op jit(solution)/shard_map/ppermute | solution.py:32
  137.5 159.1 %copy-start.13 = (f32[3,512,32]{1,2,0:T(8,128)S(1)}, f32[3,512,32]{1,2,0:T(8,128)}, u32[]{:S(2)}) copy-start(f32[3,512,32]{1,2,0:T(8,128)} %param.21) | copy-start | bytes 589828
  137.5 159.2 %copy-start.21 = (f32[3,512,32]{1,2,0:T(8,128)S(1)}, f32[3,512,32]{1,2,0:T(8,128)}, u32[]{:S(2)}) copy-start(f32[3,512,32]{1,2,0:T(8,128)} %param.24) | copy-start | bytes 589828
  137.5 159.2 %copy-start.22 = (f32[3,512,32]{1,2,0:T(8,128)S(1)}, f32[3,512,32]{1,2,0:T(8,128)}, u32[]{:S(2)}) copy-start(f32[3,512,32]{1,2,0:T(8,128)} %param.25) | copy-start | bytes 589828
  137.5 161.0 %copy-start.18 = (f32[256,64]{0,1:T(8,128)S(1)}, f32[256,64]{0,1:T(8,128)}, u32[]{:S(2)}) copy-start(f32[256,64]{0,1:T(8,128)} %param.22) | copy-start | bytes 196612
  137.5 161.0 %copy-start.24 = (f32[256,64]{0,1:T(8,128)S(1)}, f32[256,64]{0,1:T(8,128)}, u32[]{:S(2)}) copy-start(f32[256,64]{0,1:T(8,128)} %param.26) | copy-start | bytes 196612
  137.5 161.0 %copy-start.25 = (f32[256,64]{0,1:T(8,128)S(1)}, f32[256,64]{0,1:T(8,128)}, u32[]{:S(2)}) copy-start(f32[256,64]{0,1:T(8,128)} %param.27) | copy-start | bytes 196612
  137.6 162.5 %copy-start.4 = (f32[4,128,256]{2,1,0:T(8,128)S(1)}, f32[4,128,256]{2,1,0:T(8,128)}, u32[]{:S(2)}) copy-start(f32[4,128,256]{2,1,0:T(8,128)} %param.23) | copy-start | bytes 1572868
  137.6 162.5 %copy-start.14 = (f32[4,128,256]{2,1,0:T(8,128)S(1)}, f32[4,128,256]{2,1,0:T(8,128)}, u32[]{:S(2)}) copy-start(f32[4,128,256]{2,1,0:T(8,128)} %param.28) | copy-start | bytes 1572868
  137.6 162.5 %copy-start.15 = (f32[4,128,256]{2,1,0:T(8,128)S(1)}, f32[4,128,256]{2,1,0:T(8,128)}, u32[]{:S(2)}) copy-start(f32[4,128,256]{2,1,0:T(8,128)} %param.29) | copy-start | bytes 1572868
  (1 other events, 0.8 us)
Sparse Core Ops, SparseCore 0:
  10.8 58.7 all-gather.1
  129.2 157.3 all-reduce.2
where the time goes:
time: 311 us; the launch traced here: 310 us
  waiting for transfers between devices  150 us (48%)
  blocking collectives  66.4 us (21%)
  other arithmetic  48.1 us (15%)
  between operations  18.6 us (6%)
  local copies, waits for them, and re-layouts  12.2 us (4%)
  starting transfers between devices  7.34 us (2%)
  matrix products  7.32 us (2%)
    psum x1, waiting for transfers between devices, shards(): lax.psum((local_grads[0], local_grads[1], local_grads[2]), ('clip', 'tm'))  149 us
    all_gather x1, blocking collectives, shards(): lax.all_gather(pointwise_conv.astype(jnp.bfloat16), 'clip', axis=1, tiled...  33.2 us
    all_gather x1, blocking collectives, shards(): lax.all_gather(dilated_kernel_weight.astype(jnp.bfloat16), 'clip', axis=2...  33.2 us
    scatter-add x4, other arithmetic, shards(): jax.ops.segment_sum(code_grad.reshape(-1, DG), code_ids[slot].reshape(-1)...  18.6 us
    gather x4, local copies, waits for them, and re-layouts, shards(): jnp.take(table_full[slot], code_ids[slot], axis=0).astype(jnp.float32)  9.65 us
    reduce_sum x3, other arithmetic, shards(): squared = sum((jnp.sum(piece * piece) for piece in whole))  8.06 us
  transfers between devices with their start and end apart: 6, of which 2 were waited for; matrix products, arithmetic and copies ran while one was open for 4% of the time, Pallas kernels for 0%

commit v1 on v0

--- a/solution.py
+++ b/solution.py
@@ -69,9 +69,24 @@
 ):
     clip_rank = lax.axis_index("clip")
     time_rank = lax.axis_index("tm")
+
+    def pass_the_outputs(packet):
+        work_now = lax.axis_size("clip")
+        h_now = lax.axis_index("clip")
+        v_next, t1, part_next = (work_now, h_now, packet.shape[1])
+        q_next, p_next = (packet, 1)
+        while p_next < v_next:
+            copies = []
+            for dev in range(v_next):
+                copies.append((dev, (dev - p_next) % v_next))
+            parts_out = lax.ppermute(q_next, axis_name="clip", perm=copies)
+            q_next = jnp.concatenate([q_next, parts_out], axis=1)
+            p_next = 2 * p_next
+        return jnp.roll(q_next, t1 * part_next, 1)
+
     dilated_full, pointwise_full, table_full = (
         lax.all_gather(dilated_kernel_weight.astype(jnp.bfloat16), "clip", axis=2, tiled=True),
-        lax.all_gather(pointwise_conv.astype(jnp.bfloat16), "clip", axis=1, tiled=True),
+        pass_the_outputs(pointwise_conv.astype(jnp.bfloat16)),
         lax.all_gather(codebooks.astype(jnp.bfloat16), "clip", axis=1, tiled=True),
     )
     clips, frames, width = features.shape

time: 311 us -> 296 us (0.952)
  blocking collectives: 66.4 us -> 33.8 us
  waiting for transfers between devices: 150 us -> 160 us
  starting transfers between devices: 7.34 us -> 14.8 us
    all_gather x1 -> x0, blocking collectives: 33.2 us -> none  [shards(): lax.all_gather(pointwise_conv.astype(jnp.bfloat16), 'clip', axis=1, tiled...]
    ppermute x0 -> x3, waiting for transfers between devices: none -> 12.9 us  [pass_the_outputs(): parts_out = lax.ppermute(q_next, axis_name='clip', perm=copies)]
    ppermute x0 -> x3, starting transfers between devices: none -> 7.33 us  [pass_the_outputs(): parts_out = lax.ppermute(q_next, axis_name='clip', perm=copies)]
  transfers between devices with their start and end apart: 6 -> 9, of which waited for: 2 -> 3; matrix products, arithmetic and copies ran while one was open for 4% -> 4% of each run, Pallas kernels for 0% -> 0%
where the time goes in v1:
time: 296 us; the launch traced here: 295 us
  waiting for transfers between devices  160 us (54%)
  other arithmetic  47.4 us (16%)
  blocking collectives  33.8 us (11%)
  between operations  18.6 us (6%)
  starting transfers between devices  14.8 us (5%)
  local copies, waits for them, and re-layouts  12.7 us (4%)
  matrix products  7.5 us (3%)
    psum x1, waiting for transfers between devices, shards(): lax.psum((local_grads[0], local_grads[1], local_grads[2]), ('clip', 'tm'))  147 us
    all_gather x1, blocking collectives, shards(): lax.all_gather(dilated_kernel_weight.astype(jnp.bfloat16), 'clip', axis=2...  33.8 us
    scatter-add x4, other arithmetic, shards(): jax.ops.segment_sum(code_grad.reshape(-1, DG), code_ids[slot].reshape(-1)...  18.6 us
    ppermute x3, waiting for transfers between devices, pass_the_outputs(): parts_out = lax.ppermute(q_next, axis_name='clip', perm=copies)  12.9 us
    gather x4, local copies, waits for them, and re-layouts, shards(): jnp.take(table_full[slot], code_ids[slot], axis=0).astype(jnp.float32)  9.65 us
    reduce_sum x3, other arithmetic, shards(): squared = sum((jnp.sum(piece * piece) for piece in whole))  8.06 us
    ppermute x3, starting transfers between devices, pass_the_outputs(): parts_out = lax.ppermute(q_next, axis_name='clip', perm=copies)  7.33 us
  transfers between devices with their start and end apart: 9, of which 3 were waited for; matrix products, arithmetic and copies ran while one was open for 4% of the time, Pallas kernels for 0%

profile of v1, /device:TPU:0, one launch (start us, length us, event | category | flops | bytes accessed | tf_op | source)
XLA Modules:
  0.0 295.0 jit_solution(11265221258972491950)
XLA Ops:
  8.2 6.0 %collective-permute-start.2 = (bf16[256,64]{1,0:T(8,128)(2,1)S(1)}, bf16[256,64]{1,0:T(8,128)(2,1)S(1)}, u32[]{:S(2)}, u32[]{:S(2)}) collective-permute-start(bf16[256,64]{1,0:T(8,128)(2,1)S(1)} %copy.71), channel_id=1, source_target_pairs={{0,28},{4,0},{8,4},{12,8},{16,12},{20,16},{24,20},{28,24},{1,29},{... | collective-permute-start | bytes 98312 | tf_op jit(solution)/shard_map/ppermute | solution.py:82
  14.2 1.8 convert_element_type.54
  16.8 2.7 convert_multiply_fusion.1
  19.6 1.4 collective-permute-start.1
  21.0 3.0 %collective-permute-start = (bf16[2,3,512]{2,1,0:T(4,128)(2,1)S(1)}, bf16[2,3,512]{2,1,0:T(4,128)(2,1)S(1)}, u32[]{:S(2)}, u32[]{:S(2)}) collective-permute-start(bf16[2,3,512]{2,1,0:T(4,128)(2,1)S(1)} %get-tuple-element.61), channel_id=1, source_target_pairs={{0,1},{1,2},{2,3},{4,5},{5,6},{6,7},{8,9},{9,10},{10,11},{12,13},{... | collective-permute-start | bytes 18440 | tf_op jit(solution)/shard_map/ppermute | solution.py:30
  25.9 33.8 %all_gather.7 = bf16[3,512,256]{1,2,0:T(8,128)(2,1)S(1)} all-gather(bf16[3,512,32]{1,2,0:T(8,128)(2,1)S(1)} %convert_element_type.64), channel_id=1, replica_groups=mesh['clip'=8,'tm'=4] {'clip'}, dimensions={2}, use_global_device_ids=true | all-gather | bytes 884736 | tf_op jit(solution)/shard_map/all_gather | solution.py:88
  61.4 5.0 %collective-permute-done.3 = bf16[256,128]{1,0:T(8,128)(2,1)S(1)} collective-permute-done((bf16[256,128]{1,0:T(8,128)(2,1)S(1)}, bf16[256,128]{1,0:T(8,128)(2,1)S(1)}, u32[]{:S(2)}, u32[]{:S(2)}) %collective-permute-start.3) | collective-permute-done | bytes 65568 | tf_op jit(solution)/shard_map/ppermute | solution.py:82
  67.4 7.9 %collective-permute-done.4 = bf16[256,256]{1,0:T(8,128)(2,1)S(1)} collective-permute-done((bf16[256,256]{1,0:T(8,128)(2,1)S(1)}, bf16[256,256]{1,0:T(8,128)(2,1)S(1)}, u32[]{:S(2)}, u32[]{:S(2)}) %collective-permute-start.4) | collective-permute-done | bytes 131104 | tf_op jit(solution)/shard_map/ppermute | solution.py:82
  75.7 1.5 convolution_add_fusion.1
  77.2 1.7 slice_bitcast_fusion.3
  78.9 2.6 gather_fusion.1
  81.4 2.6 gather_fusion
  84.0 2.6 gather_fusion.3
  86.6 1.9 gather_fusion.2
  88.6 3.3 %fusion.12 = (f32[2,256,256]{2,1,0:T(8,128)S(1)}, f32[2,256,256]{2,1,0:T(8,128)S(1)}, f32[2,256,256]{2,1,0:T(8,128)}, f32[2,256,256]{2,1,0:T(8,128)}, f32[2,256,...) fusion(f32[2,256,512]{2,1,0:T(8,128)S(1)} %copy-done, ...), kind=kLoop, calls=%fused_computation.50 | loop fusion | flops 3932160 | bytes 7346176 | tf_op jit(solution)/shard_map/add | solution.py:119
  92.3 1.3 convolution_bitcast_fusion
  94.0 4.2 %scatter_custom_fusion.3 = f32[1024,256]{1,0:T(8,128)S(1)} fusion(s32[512]{0:T(512)S(1)} %bitcast.135, f32[512,256]{1,0:T(8,128)} %bitcast.127, f32[]{:T(128)} %constant.37.clone.1), kind=kCustom, calls=%fused_computation.74 | custom fusion | flops 131072 | bytes 1049088 | tf_op jit(solution)/shard_map/scatter-add | solution.py:122
  98.3 4.8 %scatter_custom_fusion.2 = f32[1024,256]{1,0:T(8,128)} fusion(s32[512]{0:T(512)S(1)} %bitcast.134, f32[512,256]{1,0:T(8,128)} %bitcast.126, f32[]{:T(128)} %constant.37.clone.1), kind=kCustom, calls=%fused_computation.76 | custom fusion | flops 131072 | bytes 1049088 | tf_op jit(solution)/shard_map/scatter-add | solution.py:122
  103.0 4.8 %scatter_custom_fusion.1 = f32[1024,256]{1,0:T(8,128)} fusion(s32[512]{0:T(512)S(1)} %bitcast.133, f32[512,256]{1,0:T(8,128)} %bitcast.125, f32[]{:T(128)} %constant.37.clone.1), kind=kCustom, calls=%fused_computation.78 | custom fusion | flops 131072 | bytes 1049088 | tf_op jit(solution)/shard_map/scatter-add | solution.py:122
  107.9 4.8 %scatter_custom_fusion = f32[1024,256]{1,0:T(8,128)} fusion(s32[512]{0:T(512)S(1)} %bitcast.132, f32[512,256]{1,0:T(8,128)} %bitcast.124, f32[]{:T(128)} %constant.37.clone.1), kind=kCustom, calls=%fused_computation.80 | custom fusion | flops 131072 | bytes 1049088 | tf_op jit(solution)/shard_map/scatter-add | solution.py:122
  113.4 1.3 pad_maximum_fusion.1
  114.7 2.3 pad_maximum_fusion
  117.9 1.4 collective-permute-start.6
  119.4 1.5 collective-permute-start.5
  122.5 1.6 fusion.3
  124.1 147.1 %all-reduce.3.cloned.1.call-done = (f32[3,512,256]{1,2,0:T(8,128)}, f32[256,512]{0,1:T(8,128)}, f32[4,1024,256]{2,1,0:T(8,128)}) async-done(((f32[3,512,256]{1,2,0:T(8,128)}, f32[256,512]{0,1:T(8,128)}, f32[4,1024,256]{2,1,0:T(8,128)}), (f32[3,512,256]{1,2,0:T(8,128)}, f32[256,512]{0,1:T(8,128)}, f32[4,1024,256]{2,1,0:T(8,128)})) %all-reduce.3.cloned.1.call-update) | async-done | bytes 6291472 | tf_op jit(solution)/shard_map/psum | solution.py:159
  271.2 2.4 multiply_reduce_fusion.1
  273.6 1.8 multiply_reduce_fusion.2
  275.4 3.9 %multiply_reduce_fusion = f32[]{:T(128)} fusion(f32[4,1024,256]{2,1,0:T(8,128)} %get-tuple-element.39), kind=kLoop, calls=%fused_computation.9 | loop fusion | flops 2097151 | bytes 4194308 | tf_op jit(solution)/shard_map/reduce_sum | solution.py:160
  281.3 1.8 multiply_subtract_fusion.1
  283.1 1.5 multiply_subtract_fusion.2
  284.7 2.3 multiply_subtract_fusion
  (101 shorter events, 9.6 us)
Async XLA Ops:
  7.2 18.6 %copy-start.26 = (s32[2]{0:T(128)S(1)}, s32[2]{0:T(128)}, u32[]{:S(2)}) copy-start(s32[2]{0:T(128)} %param.18) | copy-start | bytes 28
  7.2 18.7 %copy-start.23 = (s32[4,2,256]{2,1,0:T(2,128)S(1)}, s32[4,2,256]{2,1,0:T(2,128)}, u32[]{:S(2)}) copy-start(s32[4,2,256]{2,1,0:T(2,128)} %param.19) | copy-start | bytes 24580
  7.2 70.0 %all-gather.2.cloned.1.call-start = ((), (), s32[]{:S(2)}) async-start(), calls=%async_computation | async-start | bytes 2359296 | tf_op jit(solution)/shard_map/all_gather | solution.py:90
  8.2 52.0 %collective-permute-start.2 = (bf16[256,64]{1,0:T(8,128)(2,1)S(1)}, bf16[256,64]{1,0:T(8,128)(2,1)S(1)}, u32[]{:S(2)}, u32[]{:S(2)}) collective-permute-start(bf16[256,64]{1,0:T(8,128)(2,1)S(1)} %copy.71), channel_id=1, source_target_pairs={{0,28},{4,0},{8,4},{12,8},{16,12},{20,16},{24,20},{28,24},{1,29},{... | collective-permute-start | bytes 98312 | tf_op jit(solution)/shard_map/ppermute | solution.py:82
  16.0 255.2 %all-reduce.3.cloned.1.call-start = ((), (), s32[]{:S(2)}) async-start(), calls=%async_computation.1 | async-start | bytes 12582912 | tf_op jit(solution)/shard_map/psum | solution.py:159
  19.6 56.1 %copy-start.11 = (bf16[2,256,512]{2,1,0:T(8,128)(2,1)S(1)}, bf16[2,256,512]{2,1,0:T(8,128)(2,1)}, u32[]{:S(2)}) copy-start(bf16[2,256,512]{2,1,0:T(8,128)(2,1)} %param.16) | copy-start | bytes 1572868
  19.6 41.5 %collective-permute-start.1 = (bf16[2,3,512]{2,1,0:T(4,128)(2,1)S(1)}, bf16[2,3,512]{2,1,0:T(4,128)(2,1)S(1)}, u32[]{:S(2)}, u32[]{:S(2)}) collective-permute-start(bf16[2,3,512]{2,1,0:T(4,128)(2,1)S(1)} %get-tuple-element.62), channel_id=1, source_target_pairs={{1,0},{2,1},{3,2},{5,4},{6,5},{7,6},{9,8},{10,9},{11,10},{13,12},{... | collective-permute-start | bytes 18440 | tf_op jit(solution)/shard_map/ppermute | solution.py:32
  21.0 46.0 %collective-permute-start = (bf16[2,3,512]{2,1,0:T(4,128)(2,1)S(1)}, bf16[2,3,512]{2,1,0:T(4,128)(2,1)S(1)}, u32[]{:S(2)}, u32[]{:S(2)}) collective-permute-start(bf16[2,3,512]{2,1,0:T(4,128)(2,1)S(1)} %get-tuple-element.61), channel_id=1, source_target_pairs={{0,1},{1,2},{2,3},{4,5},{5,6},{6,7},{8,9},{9,10},{10,11},{12,13},{... | collective-permute-start | bytes 18440 | tf_op jit(solution)/shard_map/ppermute | solution.py:30
  60.3 6.2 %collective-permute-start.3 = (bf16[256,128]{1,0:T(8,128)(2,1)S(1)}, bf16[256,128]{1,0:T(8,128)(2,1)S(1)}, u32[]{:S(2)}, u32[]{:S(2)}) collective-permute-start(bf16[256,128]{1,0:T(8,128)(2,1)S(1)} %pad_maximum_fusion.14), channel_id=1, source_target_pairs={{0,24},{4,28},{8,0},{12,4},{16,8},{20,12},{24,16},{28,20},{1,25},{... | collective-permute-start | bytes 196616 | tf_op jit(solution)/shard_map/ppermute | solution.py:82
  66.6 8.8 %collective-permute-start.4 = (bf16[256,256]{1,0:T(8,128)(2,1)S(1)}, bf16[256,256]{1,0:T(8,128)(2,1)S(1)}, u32[]{:S(2)}, u32[]{:S(2)}) collective-permute-start(bf16[256,256]{1,0:T(8,128)(2,1)S(1)} %pad_maximum_fusion.13), channel_id=1, source_target_pairs={{0,16},{4,20},{8,24},{12,28},{16,0},{20,4},{24,8},{28,12},{1,17},{... | collective-permute-start | bytes 393224 | tf_op jit(solution)/shard_map/ppermute | solution.py:82
  67.4 9.8 %copy-start.16 = (f32[2,256,256]{2,1,0:T(8,128)}, f32[2,256,256]{2,1,0:T(8,128)S(1)}, u32[]{:S(2)}) copy-start(f32[2,256,256]{2,1,0:T(8,128)S(1)} %get-tuple-element.82) | copy-start | bytes 1572868
  84.0 4.5 %copy-start = (f32[2,256,512]{2,1,0:T(8,128)S(1)}, f32[2,256,512]{2,1,0:T(8,128)}, u32[]{:S(2)}) copy-start(f32[2,256,512]{2,1,0:T(8,128)} %get-tuple-element.77) | copy-start | bytes 3145732
  88.5 3.3 %copy-start.17 = (f32[2,256,256]{2,1,0:T(8,128)S(1)}, f32[2,256,256]{2,1,0:T(8,128)}, u32[]{:S(2)}) copy-start(f32[2,256,256]{2,1,0:T(8,128)} %copy-done.16) | copy-start | bytes 1572868
  88.5 3.3 %copy-start.19 = (bf16[256,1024]{1,0:T(8,128)(2,1)S(1)}, bf16[256,1024]{1,0:T(8,128)(2,1)}, u32[]{:S(2)}) copy-start(bf16[256,1024]{1,0:T(8,128)(2,1)} %copy-done.18) | copy-start | bytes 1572868
  91.8 2.2 copy-start.7
  91.9 2.2 copy-start.9
  117.0 4.2 %copy-start.5 = (f32[2,256,256]{2,1,0:T(8,128)S(1)}, f32[2,256,256]{2,1,0:T(8,128)}, u32[]{:S(2)}) copy-start(f32[2,256,256]{2,1,0:T(8,128)} %get-tuple-element.59) | copy-start | bytes 1572868
  117.0 4.2 %copy-start.6 = (f32[2,256,256]{2,1,0:T(8,128)S(1)}, f32[2,256,256]{2,1,0:T(8,128)}, u32[]{:S(2)}) copy-start(f32[2,256,256]{2,1,0:T(8,128)} %get-tuple-element.60) | copy-start | bytes 1572868
  117.0 5.5 %copy-start.8 = (f32[2,256,256]{2,1,0:T(8,128)S(1)}, f32[2,256,256]{2,1,0:T(8,128)}, u32[]{:S(2)}) copy-start(f32[2,256,256]{2,1,0:T(8,128)} %copy-done.7) | copy-start | bytes 1572868
  117.0 5.5 %copy-start.10 = (f32[2,256,256]{2,1,0:T(8,128)S(1)}, f32[2,256,256]{2,1,0:T(8,128)}, u32[]{:S(2)}) copy-start(f32[2,256,256]{2,1,0:T(8,128)} %copy-done.9) | copy-start | bytes 1572868
  117.9 4.6 %copy-start.12 = (bf16[2,256,512]{2,1,0:T(8,128)(2,1)S(1)}, bf16[2,256,512]{2,1,0:T(8,128)(2,1)}, u32[]{:S(2)}) copy-start(bf16[2,256,512]{2,1,0:T(8,128)(2,1)} %param.16) | copy-start | bytes 1572868
  117.9 4.2 %collective-permute-start.6 = (bf16[2,3,256]{2,1,0:T(4,128)(2,1)S(1)}, bf16[2,3,256]{2,1,0:T(4,128)(2,1)S(1)}, u32[]{:S(2)}, u32[]{:S(2)}) collective-permute-start(bf16[2,3,256]{2,1,0:T(4,128)(2,1)S(1)} %get-tuple-element.64), channel_id=1, source_target_pairs={{0,1},{1,2},{2,3},{4,5},{5,6},{6,7},{8,9},{9,10},{10,11},{12,13},{... | collective-permute-start | bytes 9224 | tf_op jit(solution)/shard_map/ppermute | solution.py:30
  119.4 3.1 %collective-permute-start.5 = (bf16[2,3,256]{2,1,0:T(4,128)(2,1)S(1)}, bf16[2,3,256]{2,1,0:T(4,128)(2,1)S(1)}, u32[]{:S(2)}, u32[]{:S(2)}) collective-permute-start(bf16[2,3,256]{2,1,0:T(4,128)(2,1)S(1)} %get-tuple-element.63), channel_id=1, source_target_pairs={{1,0},{2,1},{3,2},{5,4},{6,5},{7,6},{9,8},{10,9},{11,10},{13,12},{... | collective-permute-start | bytes 9224 | tf_op jit(solution)/shard_map/ppermute | solution.py:32
  124.1 157.2 %copy-start.13 = (f32[3,512,32]{1,2,0:T(8,128)S(1)}, f32[3,512,32]{1,2,0:T(8,128)}, u32[]{:S(2)}) copy-start(f32[3,512,32]{1,2,0:T(8,128)} %param.21) | copy-start | bytes 589828
  124.1 157.2 %copy-start.21 = (f32[3,512,32]{1,2,0:T(8,128)S(1)}, f32[3,512,32]{1,2,0:T(8,128)}, u32[]{:S(2)}) copy-start(f32[3,512,32]{1,2,0:T(8,128)} %param.24) | copy-start | bytes 589828
  124.1 157.2 %copy-start.22 = (f32[3,512,32]{1,2,0:T(8,128)S(1)}, f32[3,512,32]{1,2,0:T(8,128)}, u32[]{:S(2)}) copy-start(f32[3,512,32]{1,2,0:T(8,128)} %param.25) | copy-start | bytes 589828
  124.1 159.1 %copy-start.20 = (f32[256,64]{0,1:T(8,128)S(1)}, f32[256,64]{0,1:T(8,128)}, u32[]{:S(2)}) copy-start(f32[256,64]{0,1:T(8,128)} %param.22) | copy-start | bytes 196612
  124.1 159.1 %copy-start.24 = (f32[256,64]{0,1:T(8,128)S(1)}, f32[256,64]{0,1:T(8,128)}, u32[]{:S(2)}) copy-start(f32[256,64]{0,1:T(8,128)} %param.26) | copy-start | bytes 196612
  124.1 159.0 %copy-start.25 = (f32[256,64]{0,1:T(8,128)S(1)}, f32[256,64]{0,1:T(8,128)}, u32[]{:S(2)}) copy-start(f32[256,64]{0,1:T(8,128)} %param.27) | copy-start | bytes 196612
  124.1 160.6 %copy-start.4 = (f32[4,128,256]{2,1,0:T(8,128)S(1)}, f32[4,128,256]{2,1,0:T(8,128)}, u32[]{:S(2)}) copy-start(f32[4,128,256]{2,1,0:T(8,128)} %param.23) | copy-start | bytes 1572868
  124.1 160.6 %copy-start.14 = (f32[4,128,256]{2,1,0:T(8,128)S(1)}, f32[4,128,256]{2,1,0:T(8,128)}, u32[]{:S(2)}) copy-start(f32[4,128,256]{2,1,0:T(8,128)} %param.28) | copy-start | bytes 1572868
  124.1 160.6 %copy-start.15 = (f32[4,128,256]{2,1,0:T(8,128)S(1)}, f32[4,128,256]{2,1,0:T(8,128)}, u32[]{:S(2)}) copy-start(f32[4,128,256]{2,1,0:T(8,128)} %param.29) | copy-start | bytes 1572868
  (4 other events, 7.7 us)
Sparse Core Ops, SparseCore 0:
  16.1 57.4 all-gather.1
  117.2 153.9 all-reduce.2
